TPU v7x, 32 devices: a whole 2x2x4 slice. The times are simulated.
32 devices in a mesh: dp: 8 (over y, x, core), ctx: 4 (over z).
Axes of the slice: x: 2, y: 2, z: 4, core: 2. Of those that a mesh axis runs over, the one named last changes fastest.
Arguments:
- layer_input: bfloat16 [8, 2048, 1536], P('dp', 'ctx'), may hold values from -60 to 60
- attn_gain: bfloat16 [1536], P('dp'), may hold values from 0.5 to 1.5
- w_qkv: bfloat16 [1536, 3072], P('dp'), may hold values from -1 to 1
- w_out: bfloat16 [1536, 1536], P('dp'), may hold values from -2.5 to 2.5
- mlp_gain: bfloat16 [1536], P('dp'), may hold values from 0.5 to 1.5
- w_gate_up: bfloat16 [1536, 8192], P('dp'), may hold values from -0.15625 to 0.15625
- w_down: bfloat16 [4096, 1536], P('dp'), may hold values from -0.09375 to 0.09375
- cotangent: bfloat16 [8, 2048, 1536], P('dp', 'ctx'), may hold values from -6 to 6
Outputs:
- layer_output: bfloat16 [8, 2048, 1536], P('dp', 'ctx')
- input_grad: float32 [8, 2048, 1536], P('dp', 'ctx')
- attn_gain_grad: float32 [1536], P('dp')
- w_qkv_grad: float32 [1536, 3072], P('dp')
- w_out_grad: float32 [1536, 1536], P('dp')
- mlp_gain_grad: float32 [1536], P('dp')
- w_gate_up_grad: float32 [1536, 8192], P('dp')
- w_down_grad: float32 [4096, 1536], P('dp')
All inputs are finite; a program needn't handle non-finite values.
Results may differ from a plain program's by a relative error of at most 0.02.
Values may be sent and summed in bfloat16 or wider, within the bound.
No kernel may reach another device: no remote copies, remote signals or barrier semaphores. Data moves between devices by JAX's collectives and lax.ppermute only.
A program may use at most 256 MiB of HBM per device.

v0:
```python
import math

import jax
import jax.numpy as jnp
from jax import lax
from jax.sharding import PartitionSpec as P

H = 16
KVH = 8
HD = 96
FF = 4096


EPS = 1e-05
BASE = 100000.0


def rotate(values, cosines, sines):
    half = values.shape[-1] // 2
    first = values[..., :half]
    second = values[..., half:]
    return jnp.concatenate(
        [first * cosines - second * sines, second * cosines + first * sines], axis=-1
    )


def norm_back(inputs, inverse, gain, grad_normed):
    scaled = grad_normed * gain
    inner = jnp.mean(scaled * inputs, axis=-1, keepdims=True)
    grad_inputs = inverse * scaled - inputs * inverse * inverse * inverse * inner
    grad_gain = jnp.sum(grad_normed * inputs * inverse, axis=0)
    return (grad_inputs, grad_gain)


def reduce_grads(grads):
    shares = (
        lax.psum_scatter(
            grads[0].astype(jnp.bfloat16), "dp", scatter_dimension=0, tiled=True
        ).astype(jnp.float32),
        lax.psum_scatter(
            grads[1].astype(jnp.bfloat16), "dp", scatter_dimension=0, tiled=True
        ).astype(jnp.float32),
        lax.psum_scatter(
            grads[2].astype(jnp.bfloat16), "dp", scatter_dimension=0, tiled=True
        ).astype(jnp.float32),
    )
    return (
        lax.psum(shares[0].astype(jnp.bfloat16), "ctx").astype(jnp.float32),
        lax.psum(shares[1].astype(jnp.bfloat16), "ctx").astype(jnp.float32),
        lax.psum(shares[2].astype(jnp.bfloat16), "ctx").astype(jnp.float32),
    )


def visit_blocks(handler, carry, piece, length):
    rows = piece.shape[0]

    def visit(index, state):
        begin = index * length
        block = lax.dynamic_slice_in_dim(piece, index * length, length, 0)
        return handler(state, block, begin)

    return lax.fori_loop(0, rows // length, visit, carry)


def local(layer_input, attn_gain, w_qkv, w_out, mlp_gain, w_gate_up, w_down, cotangent):
    length = layer_input.shape[1]
    group = H // KVH
    q_width = H * HD
    kv_width = KVH * HD
    scale = 1.0 / math.sqrt(HD)
    seq_length = length * lax.axis_size("ctx")
    offset = lax.axis_index("ctx") * length
    q_pos = offset + jnp.arange(length, dtype=jnp.int32)
    q_last = offset + length - 1
    gain_a, whole_qkv, whole_out = (
        lax.all_gather(attn_gain, "dp", axis=0, tiled=True),
        lax.all_gather(w_qkv, "dp", axis=0, tiled=True),
        lax.all_gather(w_out, "dp", axis=0, tiled=True),
    )
    gain_a = gain_a.astype(jnp.float32)
    inputs = layer_input[0].astype(jnp.float32)
    inverse_a = lax.rsqrt(jnp.mean(inputs * inputs, axis=-1, keepdims=True) + EPS)
    normed_a = (inputs * inverse_a * gain_a).astype(jnp.bfloat16)
    proj = jnp.dot(normed_a, whole_qkv, preferred_element_type=jnp.float32)
    freq = BASE ** (-(jnp.arange(HD // 2, dtype=jnp.float32) * 2.0 / HD))
    angle = q_pos.astype(jnp.float32)[:, None] * freq[None, :]
    cosines = jnp.cos(angle)[:, None, :]
    sines = jnp.sin(angle)[:, None, :]
    q_rot = rotate(proj[:, :q_width].reshape(length, H, HD), cosines, sines).astype(jnp.bfloat16)
    k_rot = rotate(
        proj[:, q_width : q_width + kv_width].reshape(length, KVH, HD), cosines, sines
    ).astype(jnp.bfloat16)
    key_value = jnp.concatenate(
        [k_rot.reshape(length, kv_width), proj[:, q_width + kv_width :].astype(jnp.bfloat16)],
        axis=1,
    )
    query_heads = jnp.transpose(q_rot.reshape(length, KVH, group, HD), (1, 2, 0, 3))

    def block_scores(block, begin):
        count = block.shape[0]
        key_rows = block[:, :kv_width].reshape(count, KVH, HD)
        value_rows = block[:, kv_width:].reshape(count, KVH, HD)
        scores = (
            jnp.einsum("kgbd,tkd->kgbt", query_heads, key_rows, preferred_element_type=jnp.float32)
            * scale
        )
        key_pos = begin + jnp.arange(count, dtype=jnp.int32)
        visible = key_pos[None, :] <= q_pos[:, None]
        return (scores, visible, key_rows, value_rows)

    def forward_block(carry, block, begin):

        def forward_compute(state):
            scores, visible, key_rows, value_rows = block_scores(block, begin)
            scores = jnp.where(visible, scores, -1e30)
            top, total, mixed = state
            new_top = jnp.maximum(top, jnp.max(scores, axis=-1))
            fading = jnp.exp(top - new_top)
            weights = jnp.exp(scores - new_top[..., None])
            total = total * fading + jnp.sum(weights, axis=-1)
            mixed = mixed * fading[..., None] + jnp.einsum(
                "kgbt,tkd->kgbd",
                weights.astype(jnp.bfloat16),
                value_rows,
                preferred_element_type=jnp.float32,
            )
            return (new_top, total, mixed)

        return lax.cond(begin <= q_last, forward_compute, lambda state: state, carry)

    start_state = (
        jnp.full((KVH, group, length), -1e30, jnp.float32),
        jnp.zeros((KVH, group, length), jnp.float32),
        jnp.zeros((KVH, group, length, HD), jnp.float32),
    )
    top, total, mixed = visit_blocks(
        forward_block, start_state, lax.all_gather(key_value, "ctx", axis=0, tiled=True), length
    )
    attn_heads = mixed / total[..., None]
    log_total = top + jnp.log(total)
    attn_low = jnp.transpose(attn_heads, (2, 0, 1, 3)).reshape(length, q_width).astype(jnp.bfloat16)
    resid = inputs + jnp.dot(attn_low, whole_out, preferred_element_type=jnp.float32)
    gain_m, whole_gu, whole_down = (
        lax.all_gather(mlp_gain, "dp", axis=0, tiled=True),
        lax.all_gather(w_gate_up, "dp", axis=0, tiled=True),
        lax.all_gather(w_down, "dp", axis=0, tiled=True),
    )
    gain_m = gain_m.astype(jnp.float32)
    inverse_m = lax.rsqrt(jnp.mean(resid * resid, axis=-1, keepdims=True) + EPS)
    normed_m = (resid * inverse_m * gain_m).astype(jnp.bfloat16)
    gate_up = jnp.dot(normed_m, whole_gu, preferred_element_type=jnp.float32)
    gate = gate_up[:, :FF]
    upper = gate_up[:, FF:]
    sigmoid = jax.nn.sigmoid(gate)
    act = (gate * sigmoid * upper).astype(jnp.bfloat16)
    result = (resid + jnp.dot(act, whole_down, preferred_element_type=jnp.float32)).astype(
        jnp.bfloat16
    )
    grad_out = cotangent[0].astype(jnp.float32)
    grad_mlp = cotangent[0]
    down_grad = jnp.einsum("tf,td->fd", act, grad_mlp, preferred_element_type=jnp.float32)
    grad_act = jnp.einsum("td,fd->tf", grad_mlp, whole_down, preferred_element_type=jnp.float32)
    grad_gate = grad_act * upper * sigmoid * (1.0 + gate * (1.0 - sigmoid))
    grad_up = grad_act * gate * sigmoid
    grad_gu = jnp.concatenate([grad_gate, grad_up], axis=1).astype(jnp.bfloat16)
    gu_grad = jnp.einsum("td,tf->df", normed_m, grad_gu, preferred_element_type=jnp.float32)
    grad_nm = jnp.einsum("tf,df->td", grad_gu, whole_gu, preferred_element_type=jnp.float32)
    grad_res_m, gain_m_grad = norm_back(resid, inverse_m, gain_m, grad_nm)
    mlp_sums = reduce_grads((gain_m_grad, gu_grad, down_grad))
    grad_resid = grad_out + grad_res_m
    grad_branch = grad_resid.astype(jnp.bfloat16)
    out_grad = jnp.einsum("tc,td->cd", attn_low, grad_branch, preferred_element_type=jnp.float32)
    grad_attn = jnp.einsum(
        "td,cd->tc", grad_branch, whole_out, preferred_element_type=jnp.float32
    ).astype(jnp.bfloat16)
    grad_heads = jnp.transpose(grad_attn.reshape(length, KVH, group, HD), (1, 2, 0, 3))
    delta = jnp.sum(grad_heads.astype(jnp.float32) * attn_heads, axis=-1)

    def backward_block(carry, block, begin):

        def backward_compute(state):
            scores, visible, key_rows, value_rows = block_scores(block, begin)
            count = block.shape[0]
            probs = jnp.where(visible, jnp.exp(scores - log_total[..., None]), 0.0)
            grad_values = jnp.einsum(
                "kgbt,kgbd->tkd",
                probs.astype(jnp.bfloat16),
                grad_heads,
                preferred_element_type=jnp.float32,
            )
            grad_probs = jnp.einsum(
                "kgbd,tkd->kgbt", grad_heads, value_rows, preferred_element_type=jnp.float32
            )
            grad_scores = (probs * (grad_probs - delta[..., None])).astype(jnp.bfloat16)
            grad_query, grad_kv = state
            grad_query = (
                grad_query
                + jnp.einsum(
                    "kgbt,tkd->kgbd", grad_scores, key_rows, preferred_element_type=jnp.float32
                )
                * scale
            )
            grad_keys = (
                jnp.einsum(
                    "kgbt,kgbd->tkd", grad_scores, query_heads, preferred_element_type=jnp.float32
                )
                * scale
            )
            fresh = jnp.concatenate(
                [grad_keys.reshape(count, kv_width), grad_values.reshape(count, kv_width)], axis=1
            )
            current = lax.dynamic_slice_in_dim(grad_kv, begin, count, 0)
            return (grad_query, lax.dynamic_update_slice_in_dim(grad_kv, current + fresh, begin, 0))

        return lax.cond(begin <= q_last, backward_compute, lambda state: state, carry)

    back_state = (
        jnp.zeros((KVH, group, length, HD), jnp.float32),
        jnp.zeros((seq_length, 2 * kv_width), jnp.float32),
    )
    grad_query, grad_kv = visit_blocks(
        backward_block, back_state, lax.all_gather(key_value, "ctx", axis=0, tiled=True), length
    )
    own_kv = lax.psum_scatter(
        grad_kv.astype(jnp.bfloat16), "ctx", scatter_dimension=0, tiled=True
    ).astype(jnp.float32)
    grad_q = rotate(jnp.transpose(grad_query, (2, 0, 1, 3)).reshape(length, H, HD), cosines, -sines)
    grad_k = rotate(own_kv[:, :kv_width].reshape(length, KVH, HD), cosines, -sines)
    grad_proj = jnp.concatenate(
        [grad_q.reshape(length, q_width), grad_k.reshape(length, kv_width), own_kv[:, kv_width:]],
        axis=1,
    ).astype(jnp.bfloat16)
    qkv_grad = jnp.einsum("td,tc->dc", normed_a, grad_proj, preferred_element_type=jnp.float32)
    grad_na = jnp.einsum("tc,dc->td", grad_proj, whole_qkv, preferred_element_type=jnp.float32)
    grad_res_a, gain_a_grad = norm_back(inputs, inverse_a, gain_a, grad_na)
    input_grad = grad_resid + grad_res_a
    attn_sums = reduce_grads((gain_a_grad, qkv_grad, out_grad))
    return (
        result[None],
        input_grad[None],
        attn_sums[0],
        attn_sums[1],
        attn_sums[2],
        mlp_sums[0],
        mlp_sums[1],
        mlp_sums[2],
    )


def solution(mesh):
    return jax.shard_map(
        local,
        mesh=mesh,
        in_specs=(
            P("dp", "ctx", None),
            P("dp"),
            P("dp", None),
            P("dp", None),
            P("dp"),
            P("dp", None),
            P("dp", None),
            P("dp", "ctx", None),
        ),
        out_specs=(
            P("dp", "ctx", None),
            P("dp", "ctx", None),
            P("dp"),
            P("dp", None),
            P("dp", None),
            P("dp"),
            P("dp", None),
            P("dp", None),
        ),
        check_vma=False,
    )
```

profile of v0, /device:TPU:0, one launch (start us, length us, event | category | flops | bytes accessed | tf_op | source)
XLA Modules:
  0.0 1456.4 jit_solution(17770257266502485987)
XLA Ops:
  11.7 16.1 %all-reduce.5 = (bf16[1536]{0:T(1024)(128)(2,1)S(1)}, bf16[1536]{0:T(1024)(128)(2,1)S(1)}) all-reduce(bf16[1536]{0:T(1024)(128)(2,1)S(1)} %dynamic-update-slice, bf16[1536]{0:T(1024)(128)(2,1)S(1)} %dynamic-update-slice.1), channel_id=1, replica_groups=mesh['dp'=8,'ctx'=4] {'dp'}, use_global_device_ids=true, to_apply=%add | all-reduce | flops 3072 | bytes 12288
  30.7 40.7 %all-gather.6.cloned.1.call-done = bf16[1536,3072]{1,0:T(8,128)(2,1)} async-done(((bf16[192,3072]{1,0:T(8,128)(2,1)}), bf16[1536,3072]{1,0:T(8,128)(2,1)}) %all-gather.6.cloned.1.call-update) | async-done | bytes 9437200 | tf_op jit(solution)/shard_map/all_gather | solution.py:77
  95.5 105.0 %all-gather.8.cloned.1.call-done = bf16[2048,1536]{1,0:T(8,128)(2,1)} async-done(((bf16[512,1536]{1,0:T(8,128)(2,1)}), bf16[2048,1536]{1,0:T(8,128)(2,1)}) %all-gather.8.cloned.1.call-update) | async-done | bytes 6291472 | tf_op jit(solution)/shard_map/all_gather | solution.py:137
  209.6 30.2 %while.34 = (s32[]{:T(128)}, f32[8,2,512]{2,1,0:T(2,128)S(1)}, f32[8,2,512]{2,1,0:T(2,128)S(1)}, f32[8,2,512,96]{2,3,1,0:T(8,128)S(1)}, s32[]{:T(128)}, /*index=...) while((s32[]{:T(128)}, f32[8,2,512]{2,1,0:T(2,128)S(1)}, ...), condition=%wide.region_6.7_spmd.clone, body=%wide.region_1.6_spmd.clone.sunk | while | flops 1658602496 | bytes 64500032 | solution.py:62
  209.7 29.9 %conditional.6 = ((f32[8,2,512]{2,1,0:T(2,128)S(1)}, f32[8,2,512]{2,1,0:T(2,128)S(1)}, f32[8,2,512,96]{2,3,1,0:T(8,128)S(1)})) conditional(s32[]{:T(128)} %convert_element_type.208, (f32[8,2,512]{2,1,0:T(2,128)S(1)}, f32[8,2,512]{2,1,0:T(2,128)S(1)}, f32[8,2,512,96]{2,3,1,0:T(8,128)S(1)}) %tuple.122, (s32[]{:T(128)}, s32[]{:T(128)}, ...), branch_computations={%region_2.0_spmd, %region_3.5_spmd} | conditional | flops 1658602496 | bytes 64497760 | solution.py:129
  249.9 116.5 %all-gather.12.cloned.1.call-done = bf16[1536,8192]{1,0:T(8,128)(2,1)} async-done(((bf16[192,8192]{1,0:T(8,128)(2,1)}), bf16[1536,8192]{1,0:T(8,128)(2,1)}) %all-gather.12.cloned.1.call-update) | async-done | bytes 25165840 | tf_op jit(solution)/shard_map/all_gather | solution.py:145
  366.4 22.6 %fusion.52 = f32[512,8192]{1,0:T(8,128)} fusion(bf16[1536,8192]{1,0:T(8,128)(2,1)} %all-gather.12.cloned.1.call-done, f32[512,1536]{1,0:T(8,128)} %get-tuple-element.693, f32[1536]{0:T(1024)S(1)} %convert_element_type.152, f32[512]{0:T(512)S(1)} %add_rsqrt_fusion), kind=kOutput, calls=%fused_computation.109 | convolution fusion | flops 12887261184 | bytes 45096960 | tf_op jit(solution)/shard_map/dot_general | solution.py:151
  389.0 51.2 %all-gather.14.cloned.1.call-done = bf16[4096,1536]{1,0:T(8,128)(2,1)} async-done(((bf16[512,1536]{1,0:T(8,128)(2,1)}), bf16[4096,1536]{1,0:T(8,128)(2,1)}) %all-gather.14.cloned.1.call-update) | async-done | bytes 12582928 | tf_op jit(solution)/shard_map/all_gather | solution.py:146
  440.2 19.2 %multiply_convert_fusion.1 = (bf16[512,4096]{1,0:T(8,128)(2,1)}, bf16[512,4096]{1,0:T(8,128)(2,1)}, bf16[512,4096]{1,0:T(8,128)(2,1)}) fusion(f32[512,8192]{1,0:T(8,128)} %fusion.52, bf16[4096,1536]{1,0:T(8,128)(2,1)} %all-gather.14.cloned.1.call-done, bf16[1,512,1536]{2,1,0:T(8,128)(2,1)} %param.23), kind=kOutput, calls=%fused_computation.39 | convolution fusion | flops 6476005376 | bytes 43515904 | tf_op jit(solution)/shard_map/td,fd->tf/dot_general | solution.py:162
  459.4 21.6 %multiply_reduce_fusion = (bf16[1536]{0:T(1024)(128)(2,1)}, f32[512]{0:T(512)S(1)}, f32[512,1536]{1,0:T(8,128)}) fusion(f32[512,1536]{1,0:T(8,128)} %get-tuple-element.693, f32[512]{0:T(512)S(1)} %add_rsqrt_fusion, f32[1536]{0:T(1024)S(1)} %convert_element_type.152, bf16[1536,8192]{1,0:T(8,128)(2,1)} %all-gather.12.cloned.1.call-done, ...), kind=kOutput, calls=%fused_computation.63 | convolution fusion | flops 12906395648 | bytes 39859200 | tf_op jit(solution)/shard_map/tf,df->td/dot_general | solution.py:167
  504.8 47.5 %while.35 = (s32[]{:T(128)}, f32[8,2,512,96]{2,3,1,0:T(8,128)S(1)}, f32[2048,1536]{0,1:T(8,128)}, s32[]{:T(128)}, bf16[2048,1536]{0,1:T(8,128)(2,1)}, /*index=5*...) while((s32[]{:T(128)}, f32[8,2,512,96]{2,3,1,0:T(8,128)S(1)}, ...), condition=%wide.region_13.14_spmd.clone, body=%wide.region_10.13_spmd.clone.sunk | while | flops 4072276992 | bytes 205631968 | solution.py:62
  505.0 47.2 %conditional.7 = ((f32[8,2,512,96]{2,3,1,0:T(8,128)S(1)}, f32[2048,1536]{0,1:T(8,128)})) conditional(s32[]{:T(128)} %convert_element_type.209, (f32[8,2,512,96]{2,3,1,0:T(8,128)S(1)}, f32[2048,1536]{0,1:T(8,128)}) %tuple.125, (s32[]{:T(128)}, s32[]{:T(128)}, bf16[2048,1536]{0,1:T(8,128)(2,1)}, bf16[8,2,512,96]{2,3,1,0:T(8,128)(2,1)}, ...), branch_computations={%region_11.11_spmd, %region_12.12_spmd} | conditional | flops 4072276992 | bytes 205629664 | solution.py:215
  568.2 11.6 convolution_convert_fusion.1
  581.5 231.5 %reduce-scatter.6.cloned.1.call-done = bf16[512,1536]{0,1:T(8,128)(2,1)} async-done(((bf16[2048,1536]{0,1:T(8,128)(2,1)}), bf16[512,1536]{0,1:T(8,128)(2,1)}) %reduce-scatter.6.cloned.1.call-update) | async-done | bytes 1572880 | tf_op jit(solution)/shard_map/reduce_scatter | solution.py:224
  828.5 21.2 %convolution_convert_fusion = bf16[1536,8192]{1,0:T(8,128)(2,1)} fusion(bf16[512,4096]{1,0:T(8,128)(2,1)} %get-tuple-element.675, bf16[512,4096]{1,0:T(8,128)(2,1)} %get-tuple-element.674, f32[512,1536]{1,0:T(8,128)S(1)} %copy-done.11, f32[1536]{0:T(1024)S(1)} %copy-done.26, f32[512]{0:T(512)S(1)} %copy-done.30), kind=kOutput, calls=%fused_computation.34 | convolution fusion | flops 12916621312 | bytes 36708352 | tf_op jit(solution)/shard_map/td,tf->df/dot_general | solution.py:166
  850.0 20.8 %reduce-scatter.10.cloned.1.call-done = bf16[192,1536]{1,0:T(8,128)(2,1)} async-done(((bf16[1536,1536]{1,0:T(8,128)(2,1)}), bf16[192,1536]{1,0:T(8,128)(2,1)}) %reduce-scatter.10.cloned.1.call-update) | async-done | bytes 589840 | tf_op jit(solution)/shard_map/reduce_scatter | solution.py:43
  870.8 95.8 %reduce-scatter.14.cloned.1.call-done = bf16[512,1536]{1,0:T(8,128)(2,1)} async-done(((bf16[4096,1536]{1,0:T(8,128)(2,1)}), bf16[512,1536]{1,0:T(8,128)(2,1)}) %reduce-scatter.14.cloned.1.call-update) | async-done | bytes 1572880 | tf_op jit(solution)/shard_map/reduce_scatter | solution.py:43
  966.6 80.3 %reduce-scatter.8.cloned.1.call-done = bf16[192,3072]{1,0:T(8,128)(2,1)} async-done(((bf16[1536,3072]{1,0:T(8,128)(2,1)}), bf16[192,3072]{1,0:T(8,128)(2,1)}) %reduce-scatter.8.cloned.1.call-update) | async-done | bytes 1179664 | tf_op jit(solution)/shard_map/reduce_scatter | solution.py:40
  1046.9 159.8 %reduce-scatter.12.cloned.1.call-done = bf16[192,8192]{1,0:T(8,128)(2,1)} async-done(((bf16[1536,8192]{1,0:T(8,128)(2,1)}), bf16[192,8192]{1,0:T(8,128)(2,1)}) %reduce-scatter.12.cloned.1.call-update) | async-done | bytes 3145744 | tf_op jit(solution)/shard_map/reduce_scatter | solution.py:40
  1207.4 11.9 fusion.36
  1219.4 11.0 fusion.34
  1230.4 13.6 all-reduce.4
  1244.1 12.3 all-reduce.6
  1262.6 176.2 %all-reduce.10.cloned.1.call-done = (bf16[192,3072]{1,0:T(8,128)(2,1)}, bf16[192,1536]{1,0:T(8,128)(2,1)}, bf16[192,8192]{1,0:T(8,128)(2,1)}, bf16[512,1536]{1,0:T(8,128)(2,1)}) async-done(((bf16[192,3072]{1,0:T(8,128)(2,1)}, bf16[192,1536]{1,0:T(8,128)(2,1)}, bf16[192,8192]{1,0:T(8,128)(2,1)}, bf16[512,1536]{1,0:T(8,128)(2,1)}), (bf16[192,3072]{1,0:T(8,128)(2,1)}, bf16[192,1536]{1,0:T(8,128)(2,1)}, ...) | async-done | bytes 6488080 | tf_op jit(solution)/shard_map/psum | solution.py:49
  (177 shorter events, 201.1 us)
Async XLA Ops:
  7.2 64.2 %copy-start.6 = (bf16[1,512,1536]{2,1,0:T(8,128)(2,1)S(1)}, bf16[1,512,1536]{2,1,0:T(8,128)(2,1)}, u32[]{:S(2)}) copy-start(bf16[1,512,1536]{2,1,0:T(8,128)(2,1)} %param.16) | copy-start | bytes 4718596
  7.2 64.2 %all-gather.6.cloned.1.call-start = ((), (), s32[]{:S(2)}) async-start(), calls=%async_computation.5 | async-start | bytes 10616832 | tf_op jit(solution)/shard_map/all_gather | solution.py:77
  7.9 192.6 %all-gather.8.cloned.1.call-start = ((), (), s32[]{:S(2)}) async-start(), calls=%async_computation.6 | async-start | bytes 7864320 | tf_op jit(solution)/shard_map/all_gather | solution.py:137
  27.8 51.3 %copy-start.23 = (f32[1536]{0:T(1024)}, f32[1536]{0:T(1024)S(1)}, u32[]{:S(2)}) copy-start(f32[1536]{0:T(1024)S(1)} %convert_element_type.145) | copy-start | bytes 18436
  29.6 49.5 %copy-start.27 = (f32[512]{0:T(512)}, f32[512]{0:T(512)S(1)}, u32[]{:S(2)}) copy-start(f32[512]{0:T(512)S(1)} %add_rsqrt_fusion.1) | copy-start | bytes 6148
  30.7 63.0 %copy-start.13 = (f32[512,48]{0,1:T(8,128)}, f32[512,48]{0,1:T(8,128)S(1)}, u32[]{:S(2)}) copy-start(f32[512,48]{0,1:T(8,128)S(1)} %get-tuple-element.689) | copy-start | bytes 294916
  85.1 156.3 %all-gather.10.cloned.1.call-start = ((), (), s32[]{:S(2)}) async-start(), calls=%async_computation.7 | async-start | bytes 5308416 | tf_op jit(solution)/shard_map/all_gather | solution.py:78
  85.8 280.6 %all-gather.12.cloned.1.call-start = ((), (), s32[]{:S(2)}) async-start(), calls=%async_computation.8 | async-start | bytes 28311552 | tf_op jit(solution)/shard_map/all_gather | solution.py:145
  86.4 353.8 %all-gather.14.cloned.1.call-start = ((), (), s32[]{:S(2)}) async-start(), calls=%async_computation.9 | async-start | bytes 14155776 | tf_op jit(solution)/shard_map/all_gather | solution.py:146
  87.0 726.0 %reduce-scatter.6.cloned.1.call-start = ((), (), s32[]{:S(2)}) async-start(), calls=%async_computation.10 | async-start | bytes 7864320 | tf_op jit(solution)/shard_map/reduce_scatter | solution.py:224
  87.0 394.0 %copy-start.25 = (f32[1536]{0:T(1024)}, f32[1536]{0:T(1024)S(1)}, u32[]{:S(2)}) copy-start(f32[1536]{0:T(1024)S(1)} %convert_element_type.152) | copy-start | bytes 18436
  249.3 231.7 %copy-start.29 = (f32[512]{0:T(512)}, f32[512]{0:T(512)S(1)}, u32[]{:S(2)}) copy-start(f32[512]{0:T(512)S(1)} %add_rsqrt_fusion) | copy-start | bytes 6148
  560.6 310.2 %reduce-scatter.10.cloned.1.call-start = ((), (), s32[]{:S(2)}) async-start(), calls=%async_computation.12 | async-start | bytes 5308416 | tf_op jit(solution)/shard_map/reduce_scatter | solution.py:43
  568.1 398.5 %reduce-scatter.14.cloned.1.call-start = ((), (), s32[]{:S(2)}) async-start(), calls=%async_computation.14 | async-start | bytes 14155776 | tf_op jit(solution)/shard_map/reduce_scatter | solution.py:43
  579.9 467.1 %reduce-scatter.8.cloned.1.call-start = ((), (), s32[]{:S(2)}) async-start(), calls=%async_computation.11 | async-start | bytes 10616832 | tf_op jit(solution)/shard_map/reduce_scatter | solution.py:40
  581.4 233.6 %copy-start.15 = (bf16[512,16,96]{0,2,1:T(8,128)(2,1)}, bf16[512,16,96]{0,2,1:T(8,128)(2,1)S(1)}, u32[]{:S(2)}) copy-start(bf16[512,16,96]{0,2,1:T(8,128)(2,1)S(1)} %pad_maximum_fusion.5) | copy-start | bytes 4718596
  826.3 380.4 %reduce-scatter.12.cloned.1.call-start = ((), (), s32[]{:S(2)}) async-start(), calls=%async_computation.13 | async-start | bytes 28311552 | tf_op jit(solution)/shard_map/reduce_scatter | solution.py:40
  849.8 589.1 %all-reduce.10.cloned.1.call-start = ((), (), s32[]{:S(2)}) async-start(), calls=%async_computation.15 | async-start | bytes 12976128 | tf_op jit(solution)/shard_map/psum | solution.py:49
  1207.4 11.9 copy-start.8
  1207.4 11.9 copy-start.16
  1207.4 11.9 copy-start.20
  1207.4 11.9 copy-start.22
  1219.3 11.0 copy-start.31
  1219.3 38.2 %copy-start.5 = (f32[512,1536]{1,0:T(8,128)S(1)}, f32[512,1536]{1,0:T(8,128)}, u32[]{:S(2)}) copy-start(f32[512,1536]{1,0:T(8,128)} %copy-done.4) | copy-start | bytes 9437188
  (19 other events, 56.0 us)
Sparse Core Ops, SparseCore 0:
  9.9 61.4 all-gather.5
  85.2 115.3 all-gather.7
  202.4 36.9 all-gather.9
  241.2 125.1 all-gather.11
  368.1 71.9 all-gather.13
  560.7 252.2 reduce-scatter.5
  816.4 54.3 reduce-scatter.9
  874.3 92.2 reduce-scatter.13
  970.1 76.7 reduce-scatter.7
  1050.4 156.2 reduce-scatter.11
  1209.4 229.4 all-reduce.9
where the time goes:
time: 1460 us
  waiting for transfers between devices  1080 us (74%)
  matrix products  214 us (15%)
  other arithmetic  56.8 us (4%)
  local copies, waits for them, and re-layouts  45.9 us (3%)
  blocking collectives  42 us (3%)
  between operations  15.8 us (1%)
    reduce_scatter x2, waiting for transfers between devices, reduce_grads(): lax.psum_scatter(grads[1].astype(jnp.bfloat16), 'dp', scatter_dimension=0...  240 us
    reduce_scatter x1, waiting for transfers between devices, local(): lax.psum_scatter(grad_kv.astype(jnp.bfloat16), 'ctx', scatter_dimension=0...  232 us
    psum x1, waiting for transfers between devices, reduce_grads(): lax.psum(shares[1].astype(jnp.bfloat16), 'ctx').astype(jnp.float32)  176 us
    reduce_scatter x2, waiting for transfers between devices, reduce_grads(): lax.psum_scatter(grads[2].astype(jnp.bfloat16), 'dp', scatter_dimension=0...  117 us
    all_gather x1, waiting for transfers between devices, local(): lax.all_gather(w_gate_up, 'dp', axis=0, tiled=True)  116 us
    all_gather x1, waiting for transfers between devices, local(): lax.all_gather(key_value, 'ctx', axis=0, tiled=True)  105 us
    all_gather x1, waiting for transfers between devices, local(): lax.all_gather(w_down, 'dp', axis=0, tiled=True)  51.2 us
    all_gather x1, waiting for transfers between devices, local(): lax.all_gather(w_qkv, 'dp', axis=0, tiled=True)  40.7 us
  transfers between devices with their start and end apart: 11, of which 10 were waited for; matrix products, arithmetic and copies ran while one was open for 12% of the time, Pallas kernels for 0%

commit v1 on v0

v1 whole, which is shorter than its diff:
```python
import functools
import math

import jax
import jax.numpy as jnp
from jax import lax
from jax.experimental import pallas as pl
from jax.experimental.pallas import tpu as pltpu
from jax.sharding import PartitionSpec as P

H = 16
KVH = 8
HD = 96
FF = 4096
GROUP = H // KVH
HALF = HD // 2
Q_WIDTH = H * HD
KV_WIDTH = KVH * HD
SCALE = 1.0 / math.sqrt(HD)
LOG2_SCALE = math.log2(math.e) * SCALE


EPS = 1e-05
BASE = 100000.0
F32 = jnp.float32
BF16 = jnp.bfloat16


def dot(first, second, first_dim, second_dim):
    return lax.dot_general(
        first,
        second,
        (((first_dim,), (second_dim,)), ((), ())),
        preferred_element_type=F32,
    )


def visible(size):
    key = lax.broadcasted_iota(jnp.int32, (size, size), 0)
    query = lax.broadcasted_iota(jnp.int32, (size, size), 1)
    return key <= query


def forward_first(q_ref, k_ref, v_ref, top_ref, total_ref, mixed_ref):
    for head in range(GROUP):
        rows = pl.ds(head * HD, HD)
        scores = dot(k_ref[...], q_ref[rows, :], 0, 0)
        scores = jnp.where(visible(scores.shape[0]), scores, -1e30)
        top = jnp.max(scores, axis=0, keepdims=True)
        weights = jnp.exp2(scores * LOG2_SCALE - top * LOG2_SCALE)
        top_ref[0, head : head + 1, :] = top
        total_ref[0, head : head + 1, :] = jnp.sum(weights, axis=0, keepdims=True)
        mixed_ref[rows, :] = dot(v_ref[...], weights.astype(BF16), 1, 0)


def forward_more(flag, q_ref, k_ref, v_ref, top_in, total_in, mixed_in, top_ref, total_ref, mixed_ref):
    @pl.when(flag[0] == 1)
    def _():
        for head in range(GROUP):
            rows = pl.ds(head * HD, HD)
            scores = dot(k_ref[...], q_ref[rows, :], 0, 0)
            before = top_in[0, head : head + 1, :]
            top = jnp.maximum(jnp.max(scores, axis=0, keepdims=True), before)
            weights = jnp.exp2(scores * LOG2_SCALE - top * LOG2_SCALE)
            fading = jnp.exp2((before - top) * LOG2_SCALE)
            top_ref[0, head : head + 1, :] = top
            total_ref[0, head : head + 1, :] = (
                jnp.sum(weights, axis=0, keepdims=True)
                + total_in[0, head : head + 1, :] * fading
            )
            mixed_ref[rows, :] = (
                dot(v_ref[...], weights.astype(BF16), 1, 0) + mixed_in[rows, :] * fading
            )

    @pl.when(flag[0] != 1)
    def _():
        top_ref[...] = top_in[...]
        total_ref[...] = total_in[...]
        mixed_ref[...] = mixed_in[...]


def forward_last(
    flag, q_ref, k_ref, v_ref, top_in, total_in, mixed_in, log_ref, attn_ref, low_ref, top_s, total_s
):
    forward_more(
        flag, q_ref, k_ref, v_ref, top_in, total_in, mixed_in, top_s, total_s, attn_ref
    )
    for head in range(GROUP):
        rows = pl.ds(head * HD, HD)
        total = total_s[0, head : head + 1, :]
        attn = attn_ref[rows, :] * (1.0 / total)
        attn_ref[rows, :] = attn
        low_ref[rows, :] = attn.astype(BF16)
        log_ref[0, head : head + 1, :] = top_s[0, head : head + 1, :] * LOG2_SCALE + jnp.log2(total)


def block_specs(length):
    stat = pl.BlockSpec((1, GROUP, length), lambda g, *_: (g, 0, 0))
    wide = pl.BlockSpec((GROUP * HD, length), lambda g, *_: (g, 0))
    keys = pl.BlockSpec((HD, length), lambda g, *_: (g, 0))
    values = pl.BlockSpec((HD, length), lambda g, *_: (g + KVH, 0))
    return stat, wide, keys, values


def costs(length, products, arrays):
    return pl.CostEstimate(
        flops=2 * products * H * length * length * HD,
        bytes_accessed=arrays * Q_WIDTH * length,
        transcendentals=H * length * length,
    )


def attend_forward(queries, blocks, flags):
    length = queries.shape[1]
    stat, wide, keys, values = block_specs(length)
    stat_shape = jax.ShapeDtypeStruct((KVH, GROUP, length), F32)
    wide_shape = jax.ShapeDtypeStruct((Q_WIDTH, length), F32)
    low_shape = jax.ShapeDtypeStruct((Q_WIDTH, length), BF16)
    state = pl.pallas_call(
        forward_first,
        grid=(KVH,),
        in_specs=[wide, keys, values],
        out_specs=[stat, stat, wide],
        out_shape=[stat_shape, stat_shape, wide_shape],
        cost_estimate=costs(length, 2, 8),
        name="forward_first",
    )(queries, blocks[0], blocks[0])
    for step in range(1, len(blocks)):
        last = step == len(blocks) - 1
        state = pl.pallas_call(
            forward_last if last else forward_more,
            grid_spec=pltpu.PrefetchScalarGridSpec(
                num_scalar_prefetch=1,
                grid=(KVH,),
                in_specs=[wide, keys, values, stat, stat, wide],
                out_specs=[stat, wide, wide] if last else [stat, stat, wide],
                scratch_shapes=[pltpu.VMEM((1, GROUP, length), F32)] * 2 if last else [],
            ),
            out_shape=[stat_shape, wide_shape, low_shape]
            if last
            else [stat_shape, stat_shape, wide_shape],
            input_output_aliases={6: 1} if last else {4: 0, 5: 1, 6: 2},
            cost_estimate=costs(length, 2, 12),
            name="forward_last" if last else "forward_more",
        )(flags[step], queries, blocks[step], blocks[step], *state)
    return state


def backward_head(head, masked, q_ref, k_ref, v_ref, grad_ref, log_ref, delta):
    rows = pl.ds(head * HD, HD)
    query = q_ref[rows, :]
    grad = grad_ref[rows, :]
    scores = dot(k_ref[...], query, 0, 0)
    probs = jnp.exp2(scores * LOG2_SCALE - log_ref[0, head : head + 1, :])
    if masked:
        probs = jnp.where(visible(scores.shape[0]), probs, 0.0)
    grad_probs = dot(v_ref[...], grad, 0, 0)
    grad_scores = (probs * (grad_probs - delta)).astype(BF16)
    grad_query = dot(k_ref[...], grad_scores, 1, 0)
    grad_key = dot(query, grad_scores, 1, 1)
    grad_value = dot(grad, probs.astype(BF16), 1, 1)
    return grad_query, grad_key, grad_value


def backward_first(
    flag, q_ref, k_ref, v_ref, grad_ref, log_ref, attn_ref, delta_ref, dq_ref, dk_ref, dv_ref
):
    for head in range(GROUP):
        rows = pl.ds(head * HD, HD)
        delta_ref[0, head : head + 1, :] = jnp.sum(
            grad_ref[rows, :].astype(F32) * attn_ref[rows, :], axis=0, keepdims=True
        )

    @pl.when(flag[0] == 1)
    def _():
        for head in range(GROUP):
            rows = pl.ds(head * HD, HD)
            delta = delta_ref[0, head : head + 1, :]
            dq, dk, dv = backward_head(
                head, False, q_ref, k_ref, v_ref, grad_ref, log_ref, delta
            )
            dq_ref[rows, :] = dq
            dk_ref[...] = dk * SCALE if head == 0 else dk_ref[...] + dk * SCALE
            dv_ref[...] = dv if head == 0 else dv_ref[...] + dv

    @pl.when(flag[0] != 1)
    def _():
        dq_ref[...] = jnp.zeros_like(dq_ref)
        dk_ref[...] = jnp.zeros_like(dk_ref)
        dv_ref[...] = jnp.zeros_like(dv_ref)


def backward_more(
    masked, flag, q_ref, k_ref, v_ref, grad_ref, log_ref, delta_ref, dq_in, dq_ref, dk_ref, dv_ref
):
    @pl.when(flag[0] == 1)
    def _():
        for head in range(GROUP):
            rows = pl.ds(head * HD, HD)
            delta = delta_ref[0, head : head + 1, :]
            dq, dk, dv = backward_head(
                head, masked, q_ref, k_ref, v_ref, grad_ref, log_ref, delta
            )
            dq_ref[rows, :] = dq_in[rows, :] + dq
            dk_ref[...] = dk * SCALE if head == 0 else dk_ref[...] + dk * SCALE
            dv_ref[...] = dv if head == 0 else dv_ref[...] + dv

    @pl.when(flag[0] != 1)
    def _():
        dq_ref[...] = dq_in[...]
        dk_ref[...] = jnp.zeros_like(dk_ref)
        dv_ref[...] = jnp.zeros_like(dv_ref)


def attend_backward(queries, blocks, flags, grads, logs, attn, shift_down):
    length = queries.shape[1]
    count = len(blocks)
    stat, wide, keys, values = block_specs(length)
    stat_shape = jax.ShapeDtypeStruct((KVH, GROUP, length), F32)
    wide_shape = jax.ShapeDtypeStruct((Q_WIDTH, length), F32)
    key_shape = jax.ShapeDtypeStruct((KV_WIDTH, length), F32)
    arrived = None
    for step in range(count):
        back = count - 1 - step
        common = (flags[back], queries, blocks[back], blocks[back], grads, logs)
        if step == 0:
            delta, dq, dk, dv = pl.pallas_call(
                backward_first,
                grid_spec=pltpu.PrefetchScalarGridSpec(
                    num_scalar_prefetch=1,
                    grid=(KVH,),
                    in_specs=[wide, keys, values, wide, stat, wide],
                    out_specs=[stat, wide, keys, keys],
                ),
                out_shape=[stat_shape, wide_shape, key_shape, key_shape],
                cost_estimate=costs(length, 5, 20),
                name="backward_first",
            )(*common, attn)
        else:
            dq, dk, dv = pl.pallas_call(
                functools.partial(backward_more, back == 0),
                grid_spec=pltpu.PrefetchScalarGridSpec(
                    num_scalar_prefetch=1,
                    grid=(KVH,),
                    in_specs=[wide, keys, values, wide, stat, stat, wide],
                    out_specs=[wide, keys, keys],
                ),
                out_shape=[wide_shape, key_shape, key_shape],
                input_output_aliases={7: 0},
                cost_estimate=costs(length, 5, 20),
                name="backward_more",
            )(*common, delta, dq)
        fresh = jnp.concatenate([dk, dv], axis=0)
        if arrived is not None:
            fresh = fresh + arrived.astype(F32)
        if back > 0:
            arrived = shift_down(fresh.astype(BF16))
    return dq, fresh


def rotate(values, cosines, sines):
    parts = values.reshape(-1, 2, HALF, values.shape[1])
    first = parts[:, 0]
    second = parts[:, 1]
    return jnp.stack(
        [first * cosines - second * sines, second * cosines + first * sines], axis=1
    ).reshape(values.shape)


def norm_back(inputs, inverse, gain, grad_normed):
    scaled = grad_normed * gain
    inner = jnp.mean(scaled * inputs, axis=-1, keepdims=True)
    grad_inputs = inverse * scaled - inputs * inverse * inverse * inverse * inner
    grad_gain = jnp.sum(grad_normed * inputs * inverse, axis=0)
    return (grad_inputs, grad_gain)


def sum_over_ctx(share):
    count = lax.axis_size("ctx")
    place = lax.axis_index("ctx")
    bits = []
    distance = 1
    value = share
    while distance < count:
        rows = value.shape[0] // 2
        bit = (place // distance) % 2
        perm = [(i, i ^ distance) for i in range(count)]
        away = lax.dynamic_slice_in_dim(value, (1 - bit) * rows, rows, 0)
        keep = lax.dynamic_slice_in_dim(value, bit * rows, rows, 0)
        got = lax.ppermute(away, "ctx", perm)
        value = (keep.astype(F32) + got.astype(F32)).astype(BF16)
        bits.append((bit, perm))
        distance *= 2
    for bit, perm in reversed(bits):
        got = lax.ppermute(value, "ctx", perm)
        low = jnp.where(bit == 0, value, got)
        high = jnp.where(bit == 0, got, value)
        value = jnp.concatenate([low, high], axis=0)
    return value.astype(F32)


def local(layer_input, attn_gain, w_qkv, w_out, mlp_gain, w_gate_up, w_down, cotangent):
    length = layer_input.shape[1]
    count = lax.axis_size("ctx")
    place = lax.axis_index("ctx")
    up = [(i, i + 1) for i in range(count - 1)]
    down = [(i + 1, i) for i in range(count - 1)]

    def gather(shard):
        return lax.all_gather(shard, "dp", axis=0, tiled=True)

    def scatter(grad):
        return lax.psum_scatter(grad.astype(BF16), "dp", scatter_dimension=0, tiled=True)

    whole_kv = gather(w_qkv[:, Q_WIDTH:])
    whole_q = gather(w_qkv[:, :Q_WIDTH])
    whole_out = gather(w_out)
    whole_gu = gather(w_gate_up)
    whole_down = gather(w_down)
    gain_a = gather(attn_gain).astype(F32)
    gain_m = gather(mlp_gain).astype(F32)

    q_pos = place * length + jnp.arange(length, dtype=jnp.int32)
    freq = BASE ** (-(jnp.arange(HALF, dtype=F32) * 2.0 / HD))
    angle = freq[:, None] * q_pos.astype(F32)[None, :]
    cosines = jnp.cos(angle)
    sines = jnp.sin(angle)

    inputs = layer_input[0].astype(F32)
    inverse_a = lax.rsqrt(jnp.mean(inputs * inputs, axis=-1, keepdims=True) + EPS)
    normed_a = (inputs * inverse_a * gain_a).astype(BF16)

    proj_kv = dot(whole_kv, normed_a, 0, 1)
    k_rot = rotate(proj_kv[:KV_WIDTH], cosines, sines).astype(BF16)
    key_value = jnp.concatenate([k_rot, proj_kv[KV_WIDTH:].astype(BF16)], axis=0)
    blocks = [key_value]
    for _ in range(count - 1):
        blocks.append(lax.ppermute(blocks[-1], "ctx", up))
    flags = [(place >= step).astype(jnp.int32).reshape(1) for step in range(count)]
    q_rot = rotate(dot(whole_q, normed_a, 0, 1), cosines, sines).astype(BF16)

    logs, attn, attn_low = attend_forward(q_rot, blocks, flags)
    resid = inputs + dot(attn_low, whole_out, 0, 0)

    inverse_m = lax.rsqrt(jnp.mean(resid * resid, axis=-1, keepdims=True) + EPS)
    normed_m = (resid * inverse_m * gain_m).astype(BF16)
    gate_up = dot(normed_m, whole_gu, 1, 0)
    gate = gate_up[:, :FF]
    upper = gate_up[:, FF:]
    sigmoid = jax.nn.sigmoid(gate)
    act = (gate * sigmoid * upper).astype(BF16)
    grad_out = cotangent[0].astype(F32)
    grad_mlp = cotangent[0]
    down_share = scatter(dot(act, grad_mlp, 0, 0))
    result = (resid + dot(act, whole_down, 1, 0)).astype(BF16)
    grad_act = dot(grad_mlp, whole_down, 1, 1)
    grad_gate = grad_act * upper * sigmoid * (1.0 + gate * (1.0 - sigmoid))
    grad_up = grad_act * gate * sigmoid
    grad_gu = jnp.concatenate([grad_gate, grad_up], axis=1).astype(BF16)
    gu_share = scatter(dot(normed_m, grad_gu, 0, 0))
    grad_nm = dot(grad_gu, whole_gu, 1, 1)
    grad_res_m, gain_m_grad = norm_back(resid, inverse_m, gain_m, grad_nm)
    grad_resid = grad_out + grad_res_m
    grad_branch = grad_resid.astype(BF16)
    out_share = scatter(dot(attn_low, grad_branch, 1, 0))
    grad_attn = dot(whole_out, grad_branch, 1, 1).astype(BF16)

    grad_query, grad_kv = attend_backward(
        q_rot, blocks, flags, grad_attn, logs, attn, lambda x: lax.ppermute(x, "ctx", down)
    )
    gproj_q = rotate(grad_query * SCALE, cosines, -sines).astype(BF16)
    q_share = scatter(dot(normed_a, gproj_q, 0, 1))
    gproj_kv = jnp.concatenate(
        [rotate(grad_kv[:KV_WIDTH], cosines, -sines), grad_kv[KV_WIDTH:]], axis=0
    ).astype(BF16)
    kv_share = scatter(dot(normed_a, gproj_kv, 0, 1))
    grad_na = dot(gproj_q, whole_q, 0, 1) + dot(gproj_kv, whole_kv, 0, 1)
    grad_res_a, gain_a_grad = norm_back(inputs, inverse_a, gain_a, grad_na)
    input_grad = grad_resid + grad_res_a

    gains = lax.psum(jnp.stack([gain_a_grad, gain_m_grad]), ("dp", "ctx"))
    rows = attn_gain.shape[0]
    gains = lax.dynamic_slice_in_dim(gains, lax.axis_index("dp") * rows, rows, 1)
    return (
        result[None],
        input_grad[None],
        gains[0],
        jnp.concatenate([sum_over_ctx(q_share), sum_over_ctx(kv_share)], axis=1),
        sum_over_ctx(out_share),
        gains[1],
        sum_over_ctx(gu_share),
        sum_over_ctx(down_share),
    )


def solution(mesh):
    return jax.shard_map(
        local,
        mesh=mesh,
        in_specs=(
            P("dp", "ctx", None),
            P("dp"),
            P("dp", None),
            P("dp", None),
            P("dp"),
            P("dp", None),
            P("dp", None),
            P("dp", "ctx", None),
        ),
        out_specs=(
            P("dp", "ctx", None),
            P("dp", "ctx", None),
            P("dp"),
            P("dp", None),
            P("dp", None),
            P("dp"),
            P("dp", None),
            P("dp", None),
        ),
        check_vma=False,
    )
```

time: 1460 us -> 1120 us (0.77)
  waiting for transfers between devices: 1080 us -> 694 us
  Pallas kernels: 0 us -> 72.3 us
  matrix products: 214 us -> 164 us
  starting transfers between devices: 1.02 us -> 44.1 us
  local copies, waits for them, and re-layouts: 45.9 us -> 23.6 us
  other arithmetic: 56.8 us -> 39.2 us
    reduce_scatter x5, waiting for transfers between devices: 588 us -> 208 us  [scatter(): lax.psum_scatter(grad.astype(BF16), 'dp', scatter_dimension=0, tiled=True)]
    ppermute x0 -> x26, waiting for transfers between devices: none -> 340 us  [the longest x10 101 us: sum_over_ctx(): got = lax.ppermute(away, 'ctx', perm)]
    psum x1 -> x0, waiting for transfers between devices: 176 us -> none  [reduce_grads(): lax.psum(shares[1].astype(jnp.bfloat16), 'ctx').astype(jnp.float32)]
    all_gather x5, waiting for transfers between devices: 313 us -> 144 us  [gather(): return lax.all_gather(shard, 'dp', axis=0, tiled=True)]
    pallas_call x0 -> x8, Pallas kernels: none -> 72.3 us  [the longest x3 31.8 us: attend_backward(): pl.pallas_call(functools.partial(backward_more, back == 0), grid_spec=plt...]
    dot_general x19 -> x15, matrix products: 214 us -> 164 us  [dot(): lax.dot_general(first, second, (((first_dim,), (second_dim,)), ((), ())),...]
    ppermute x0 -> x26, starting transfers between devices: none -> 43.7 us  [the longest x3 15.8 us: local(): blocks.append(lax.ppermute(blocks[-1], 'ctx', up))]
    psum x1, blocking collectives: 12.3 us -> 40.4 us  [local(): gains = lax.psum(jnp.stack([gain_a_grad, gain_m_grad]), ('dp', 'ctx'))]
  transfers between devices with their start and end apart: 11 -> 36, of which waited for: 10 -> 21; matrix products, arithmetic and copies ran while one was open for 12% -> 14% of each run, Pallas kernels for 0% -> 6%
where the time goes in v1:
time: 1120 us; the launch traced here: 1110 us
  waiting for transfers between devices  694 us (62%)
  matrix products  164 us (15%)
  Pallas kernels  72.3 us (6%)
  blocking collectives  56.5 us (5%)
  starting transfers between devices  44.1 us (4%)
  other arithmetic  39.2 us (4%)
  local copies, waits for them, and re-layouts  23.6 us (2%)
  between operations  15.8 us (1%)
    reduce_scatter x5, waiting for transfers between devices, scatter(): lax.psum_scatter(grad.astype(BF16), 'dp', scatter_dimension=0, tiled=True)  208 us
    dot_general x15, matrix products, dot(): lax.dot_general(first, second, (((first_dim,), (second_dim,)), ((), ())),...  164 us
    all_gather x5, waiting for transfers between devices, gather(): return lax.all_gather(shard, 'dp', axis=0, tiled=True)  144 us
    ppermute x10, waiting for transfers between devices, sum_over_ctx(): got = lax.ppermute(away, 'ctx', perm)  101 us
    ppermute x10, waiting for transfers between devices, sum_over_ctx(): got = lax.ppermute(value, 'ctx', perm)  93 us
    ppermute x3, waiting for transfers between devices, local(): lax.ppermute(x, 'ctx', down)  80.9 us
    ppermute x3, waiting for transfers between devices, local(): blocks.append(lax.ppermute(blocks[-1], 'ctx', up))  65.2 us
    psum x1, blocking collectives, local(): gains = lax.psum(jnp.stack([gain_a_grad, gain_m_grad]), ('dp', 'ctx'))  40.4 us
  transfers between devices with their start and end apart: 36, of which 21 were waited for; matrix products, arithmetic and copies ran while one was open for 14% of the time, Pallas kernels for 6%

profile of v1, /device:TPU:0, one launch (start us, length us, event | category | flops | bytes accessed | tf_op | source)
XLA Modules:
  0.0 1109.5 jit_solution(5803589022310184845)
XLA Ops:
  14.1 16.1 %all-reduce.2 = (bf16[1536]{0:T(1024)(128)(2,1)S(1)}, bf16[1536]{0:T(1024)(128)(2,1)S(1)}) all-reduce(bf16[1536]{0:T(1024)(128)(2,1)S(1)} %dynamic-update-slice, bf16[1536]{0:T(1024)(128)(2,1)S(1)} %dynamic-update-slice.1), channel_id=1, replica_groups=mesh['dp'=8,'ctx'=4] {'dp'}, use_global_device_ids=true, to_apply=%add | all-reduce | flops 3072 | bytes 12288
  31.1 21.1 %all-gather.8.cloned.1.call-done = bf16[1536,1536]{1,0:T(8,128)(2,1)} async-done(((bf16[192,1536]{1,0:T(8,128)(2,1)}), bf16[1536,1536]{1,0:T(8,128)(2,1)}) %all-gather.8.cloned.1.call-update) | async-done | bytes 4718608 | tf_op jit(solution)/shard_map/all_gather | solution.py:310
  62.2 32.9 %collective-permute-done.k_ref.v_ref = bf16[1536,512]{1,0:T(8,128)(2,1)} collective-permute-done((bf16[1536,512]{1,0:T(8,128)(2,1)S(1)}, bf16[1536,512]{1,0:T(8,128)(2,1)}, u32[]{:S(2)}, u32[]{:S(2)}) %collective-permute-start) | collective-permute-done | bytes 1572896 | tf_op jit(solution)/shard_map/ppermute | solution.py:338
  100.7 32.3 %collective-permute-done.1.k_ref.v_ref = bf16[1536,512]{1,0:T(8,128)(2,1)} collective-permute-done((bf16[1536,512]{1,0:T(8,128)(2,1)}, bf16[1536,512]{1,0:T(8,128)(2,1)}, u32[]{:S(2)}, u32[]{:S(2)}) %collective-permute-start.1) | collective-permute-done | bytes 1572896 | tf_op jit(solution)/shard_map/ppermute | solution.py:338
  190.1 71.0 %all-gather.12.cloned.1.call-done = bf16[1536,8192]{1,0:T(8,128)(2,1)} async-done(((bf16[192,8192]{1,0:T(8,128)(2,1)}), bf16[1536,8192]{1,0:T(8,128)(2,1)}) %all-gather.12.cloned.1.call-update) | async-done | bytes 25165840 | tf_op jit(solution)/shard_map/all_gather | solution.py:310
  261.1 22.3 %fusion.39 = f32[512,8192]{1,0:T(8,128)} fusion(bf16[1536,8192]{1,0:T(8,128)(2,1)} %all-gather.12.cloned.1.call-done, f32[512,1536]{1,0:T(8,128)} %get-tuple-element.103, f32[1536]{0:T(1024)S(1)} %convert_element_type.216, f32[512]{0:T(512)S(1)} %add_rsqrt_fusion), kind=kOutput, calls=%fused_computation.140 | convolution fusion | flops 12887261184 | bytes 45096960 | tf_op jit(solution)/shard_map/dot_general | solution.py:30
  283.4 51.4 %all-gather.14.cloned.1.call-done = bf16[4096,1536]{1,0:T(8,128)(2,1)} async-done(((bf16[512,1536]{1,0:T(8,128)(2,1)}), bf16[4096,1536]{1,0:T(8,128)(2,1)}) %all-gather.14.cloned.1.call-update) | async-done | bytes 12582928 | tf_op jit(solution)/shard_map/all_gather | solution.py:310
  334.9 19.7 %multiply_convert_fusion.1 = (bf16[512,4096]{1,0:T(8,128)(2,1)}, bf16[512,4096]{1,0:T(8,128)(2,1)}, bf16[512,4096]{1,0:T(8,128)(2,1)}) fusion(f32[512,8192]{1,0:T(8,128)} %fusion.39, bf16[4096,1536]{1,0:T(8,128)(2,1)} %all-gather.14.cloned.1.call-done, bf16[1,512,1536]{2,1,0:T(8,128)(2,1)} %param.15), kind=kOutput, calls=%fused_computation.4 | convolution fusion | flops 6476005376 | bytes 43515904 | tf_op jit(solution)/shard_map/dot_general | solution.py:30
  354.6 21.0 %multiply_reduce_fusion = (f32[1536]{0:T(1024)S(1)}, f32[512]{0:T(512)S(1)}, f32[512,1536]{1,0:T(8,128)}) fusion(f32[512,1536]{1,0:T(8,128)S(1)} %copy-done.8, f32[512]{0:T(512)S(1)} %add_rsqrt_fusion, f32[1536]{0:T(1024)S(1)} %convert_element_type.216, bf16[1536,8192]{1,0:T(8,128)(2,1)} %all-gather.12.cloned.1.call-done, ...), kind=kOutput, calls=%fused_computation.44 | convolution fusion | flops 12906395648 | bytes 39862272 | tf_op jit(solution)/shard_map/dot_general | solution.py:30
  413.0 24.6 %collective-permute-done.3 = bf16[1536,512]{1,0:T(8,128)(2,1)} collective-permute-done((bf16[1536,512]{1,0:T(8,128)(2,1)}, bf16[1536,512]{1,0:T(8,128)(2,1)}, u32[]{:S(2)}, u32[]{:S(2)}) %collective-permute-start.3) | collective-permute-done | bytes 1572896 | tf_op jit(solution)/shard_map/ppermute | solution.py:369
  450.0 28.5 %collective-permute-done.4 = bf16[1536,512]{1,0:T(8,128)(2,1)S(1)} collective-permute-done((bf16[1536,512]{1,0:T(8,128)(2,1)S(1)}, bf16[1536,512]{1,0:T(8,128)(2,1)S(1)}, u32[]{:S(2)}, u32[]{:S(2)}) %collective-permute-start.4) | collective-permute-done | bytes 1572896 | tf_op jit(solution)/shard_map/ppermute | solution.py:369
  483.9 15.3 %backward_more.5 = (f32[1536,512]{1,0:T(8,128)}, f32[768,512]{1,0:T(8,128)}, f32[768,512]{1,0:T(8,128)}) custom-call(s32[1]{0:T(128)} %bitcast.13.flag, bf16[1536,512]{1,0:T(8,128)(2,1)} %bitcast.105, bf16[1536,512]{1,0:T(8,128)(2,1)} %copy-done.14, bf16[1536,512]{1,0:T(8,128)(2,1)} %copy-done.14, ...), custom_call_target="tpu_custom_call", output_to_operand_aliasing={{0}: (7, {})} | custom-call | flops 4026531840 | bytes 15728640 | tf_op jit(solution)/shard_map/backward_more/pallas_call | solution.py:240
  499.2 27.8 %collective-permute-done.5 = bf16[1536,512]{1,0:T(8,128)(2,1)S(1)} collective-permute-done((bf16[1536,512]{1,0:T(8,128)(2,1)S(1)}, bf16[1536,512]{1,0:T(8,128)(2,1)S(1)}, u32[]{:S(2)}, u32[]{:S(2)}) %collective-permute-start.5) | collective-permute-done | bytes 1572896 | tf_op jit(solution)/shard_map/ppermute | solution.py:369
  548.5 12.6 %convolution_convert_fusion.1 = bf16[4096,1536]{1,0:T(8,128)(2,1)} fusion(bf16[512,4096]{1,0:T(8,128)(2,1)} %get-tuple-element.66, bf16[1,512,1536]{2,1,0:T(8,128)(2,1)S(1)} %copy-done.17), kind=kOutput, calls=%fused_computation.1 | convolution fusion | flops 6448742400 | bytes 18350080 | tf_op jit(solution)/shard_map/dot_general | solution.py:30
  563.7 20.8 %convolution_convert_fusion = bf16[1536,8192]{1,0:T(8,128)(2,1)} fusion(bf16[512,4096]{1,0:T(8,128)(2,1)} %get-tuple-element.65, bf16[512,4096]{1,0:T(8,128)(2,1)} %get-tuple-element.64, f32[512,1536]{1,0:T(8,128)S(1)} %copy-done.9, f32[1536]{0:T(1024)S(1)} %convert_element_type.216, f32[512]{0:T(512)S(1)} %add_rsqrt_fusion), kind=kOutput, calls=%fused_computation | convolution fusion | flops 12916621312 | bytes 36708352 | tf_op jit(solution)/shard_map/dot_general | solution.py:30
  630.9 40.4 %psum.7 = f32[2,1536]{1,0:T(2,128)S(1)} all-reduce(f32[2,1536]{1,0:T(2,128)S(1)} %pad_maximum_fusion.16), channel_id=1, replica_groups=mesh['dp'=8,'ctx'=4] {'dp','ctx'}, use_global_device_ids=true, to_apply=%region_6.0 | all-reduce | flops 3072 | bytes 24576 | tf_op jit(solution)/shard_map/psum | solution.py:381
  695.5 51.0 %reduce-scatter.14.cloned.1.call-done = bf16[512,1536]{1,0:T(8,128)(2,1)} async-done(((bf16[4096,1536]{1,0:T(8,128)(2,1)}), bf16[512,1536]{1,0:T(8,128)(2,1)}) %reduce-scatter.14.cloned.1.call-update) | async-done | bytes 1572880 | tf_op jit(solution)/shard_map/reduce_scatter | solution.py:313
  749.4 156.9 %reduce-scatter.12.cloned.1.call-done = bf16[192,8192]{1,0:T(8,128)(2,1)} async-done(((bf16[1536,8192]{1,0:T(8,128)(2,1)}), bf16[192,8192]{1,0:T(8,128)(2,1)}) %reduce-scatter.12.cloned.1.call-update) | async-done | bytes 3145744 | tf_op jit(solution)/shard_map/reduce_scatter | solution.py:313
  915.6 41.1 %collective-permute-done.18 = bf16[96,8192]{1,0:T(8,128)(2,1)S(1)} collective-permute-done((bf16[96,8192]{1,0:T(8,128)(2,1)S(1)}, bf16[96,8192]{1,0:T(8,128)(2,1)S(1)}, u32[]{:S(2)}, u32[]{:S(2)}) %collective-permute-start.18) | collective-permute-done | bytes 1572896 | tf_op jit(solution)/shard_map/ppermute | solution.py:290
  965.7 40.1 %collective-permute-done.19 = bf16[48,8192]{1,0:T(8,128)(2,1)S(1)} collective-permute-done((bf16[48,8192]{1,0:T(8,128)(2,1)S(1)}, bf16[48,8192]{1,0:T(8,128)(2,1)S(1)}, u32[]{:S(2)}, u32[]{:S(2)}) %collective-permute-start.19) | collective-permute-done | bytes 786464 | tf_op jit(solution)/shard_map/ppermute | solution.py:290
  1006.2 24.9 %collective-permute-done.24 = bf16[128,1536]{1,0:T(8,128)(2,1)S(1)} collective-permute-done((bf16[128,1536]{1,0:T(8,128)(2,1)S(1)}, bf16[128,1536]{1,0:T(8,128)(2,1)S(1)}, u32[]{:S(2)}, u32[]{:S(2)}) %collective-permute-start.24) | collective-permute-done | bytes 393248 | tf_op jit(solution)/shard_map/ppermute | solution.py:295
  1031.3 16.7 %collective-permute-done.20 = bf16[48,8192]{1,0:T(8,128)(2,1)S(1)} collective-permute-done((bf16[48,8192]{1,0:T(8,128)(2,1)S(1)}, bf16[48,8192]{1,0:T(8,128)(2,1)S(1)}, u32[]{:S(2)}, u32[]{:S(2)}) %collective-permute-start.20) | collective-permute-done | bytes 786464 | tf_op jit(solution)/shard_map/ppermute | solution.py:295
  1050.1 14.7 %collective-permute-done.25 = bf16[256,1536]{1,0:T(8,128)(2,1)S(1)} collective-permute-done((bf16[256,1536]{1,0:T(8,128)(2,1)S(1)}, bf16[256,1536]{1,0:T(8,128)(2,1)S(1)}, u32[]{:S(2)}, u32[]{:S(2)}) %collective-permute-start.25) | collective-permute-done | bytes 786464 | tf_op jit(solution)/shard_map/ppermute | solution.py:295
  1067.2 31.3 %collective-permute-done.21 = bf16[96,8192]{1,0:T(8,128)(2,1)S(1)} collective-permute-done((bf16[96,8192]{1,0:T(8,128)(2,1)S(1)}, bf16[96,8192]{1,0:T(8,128)(2,1)S(1)}, u32[]{:S(2)}, u32[]{:S(2)}) %collective-permute-start.21) | collective-permute-done | bytes 1572896 | tf_op jit(solution)/shard_map/ppermute | solution.py:295
  (220 shorter events, 259.0 us)
Async XLA Ops:
  7.2 45.0 %all-gather.8.cloned.1.call-start = ((), (), s32[]{:S(2)}) async-start(), calls=%async_computation.6 | async-start | bytes 5308416 | tf_op jit(solution)/shard_map/all_gather | solution.py:310
  9.6 129.0 %all-gather.6.cloned.1.call-start = ((), (), s32[]{:S(2)}) async-start(), calls=%async_computation.5 | async-start | bytes 5308416 | tf_op jit(solution)/shard_map/all_gather | solution.py:310
  10.3 172.0 %all-gather.10.cloned.1.call-start = ((), (), s32[]{:S(2)}) async-start(), calls=%async_computation.7 | async-start | bytes 5308416 | tf_op jit(solution)/shard_map/all_gather | solution.py:310
  11.1 250.0 %all-gather.12.cloned.1.call-start = ((), (), s32[]{:S(2)}) async-start(), calls=%async_computation.8 | async-start | bytes 28311552 | tf_op jit(solution)/shard_map/all_gather | solution.py:310
  11.6 323.2 %all-gather.14.cloned.1.call-start = ((), (), s32[]{:S(2)}) async-start(), calls=%async_computation.9 | async-start | bytes 14155776 | tf_op jit(solution)/shard_map/all_gather | solution.py:310
  12.2 591.6 %reduce-scatter.10.cloned.1.call-start = ((), (), s32[]{:S(2)}) async-start(), calls=%async_computation.12 | async-start | bytes 5308416 | tf_op jit(solution)/shard_map/reduce_scatter | solution.py:313
  133.0 41.6 %collective-permute-start.2 = (bf16[1536,512]{1,0:T(8,128)(2,1)}, bf16[1536,512]{1,0:T(8,128)(2,1)}, u32[]{:S(2)}, u32[]{:S(2)}) collective-permute-start(bf16[1536,512]{1,0:T(8,128)(2,1)} %collective-permute-done.1.k_ref.v_ref), channel_id=1, source_target_pairs={{0,1},{1,2},{2,3},{4,5},{5,6},{6,7},{8,9},{9,10},{10,11},{12,13},{... | collective-permute-start | bytes 4718600 | tf_op jit(solution)/shard_map/ppermute | solution.py:338
  404.7 267.4 %reduce-scatter.8.cloned.1.call-start = ((), (), s32[]{:S(2)}) async-start(), calls=%async_computation.11 | async-start | bytes 5308416 | tf_op jit(solution)/shard_map/reduce_scatter | solution.py:313
  482.6 44.4 %collective-permute-start.5 = (bf16[1536,512]{1,0:T(8,128)(2,1)S(1)}, bf16[1536,512]{1,0:T(8,128)(2,1)S(1)}, u32[]{:S(2)}, u32[]{:S(2)}) collective-permute-start(bf16[1536,512]{1,0:T(8,128)(2,1)S(1)} %fusion.20), channel_id=1, source_target_pairs={{1,0},{2,1},{3,2},{5,4},{6,5},{7,6},{9,8},{10,9},{11,10},{13,12},{... | collective-permute-start | bytes 4718600 | tf_op jit(solution)/shard_map/ppermute | solution.py:369
  540.0 134.5 %reduce-scatter.6.cloned.1.call-start = ((), (), s32[]{:S(2)}) async-start(), calls=%async_computation.10 | async-start | bytes 5308416 | tf_op jit(solution)/shard_map/reduce_scatter | solution.py:313
  546.9 199.6 %reduce-scatter.14.cloned.1.call-start = ((), (), s32[]{:S(2)}) async-start(), calls=%async_computation.14 | async-start | bytes 14155776 | tf_op jit(solution)/shard_map/reduce_scatter | solution.py:313
  561.1 345.2 %reduce-scatter.12.cloned.1.call-start = ((), (), s32[]{:S(2)}) async-start(), calls=%async_computation.13 | async-start | bytes 28311552 | tf_op jit(solution)/shard_map/reduce_scatter | solution.py:313
  691.9 217.5 %collective-permute-start.7 = (bf16[48,1536]{1,0:T(8,128)(2,1)}, bf16[48,1536]{1,0:T(8,128)(2,1)}, u32[]{:S(2)}, u32[]{:S(2)}) collective-permute-start(bf16[48,1536]{1,0:T(8,128)(2,1)} %constant_dynamic-slice_fusion.9), channel_id=1, source_target_pairs={{0,2},{1,3},{2,0},{3,1},{4,6},{5,7},{6,4},{7,5},{8,10},{9,11},{10,... | collective-permute-start | bytes 442376 | tf_op jit(solution)/shard_map/ppermute | solution.py:290
  692.7 220.1 %collective-permute-start.12 = (bf16[48,1536]{1,0:T(8,128)(2,1)}, bf16[48,1536]{1,0:T(8,128)(2,1)}, u32[]{:S(2)}, u32[]{:S(2)}) collective-permute-start(bf16[48,1536]{1,0:T(8,128)(2,1)} %add_convert_fusion.11), channel_id=1, source_target_pairs={{0,2},{1,3},{2,0},{3,1},{4,6},{5,7},{6,4},{7,5},{8,10},{9,11},{10,... | collective-permute-start | bytes 442376 | tf_op jit(solution)/shard_map/ppermute | solution.py:295
  747.8 167.0 %collective-permute-start.22 = (bf16[256,1536]{1,0:T(8,128)(2,1)S(1)}, bf16[256,1536]{1,0:T(8,128)(2,1)S(1)}, u32[]{:S(2)}, u32[]{:S(2)}) collective-permute-start(bf16[256,1536]{1,0:T(8,128)(2,1)S(1)} %constant_dynamic-slice_fusion.2), channel_id=1, source_target_pairs={{0,1},{1,0},{2,3},{3,2},{4,5},{5,4},{6,7},{7,6},{8,9},{9,8},{10,11... | collective-permute-start | bytes 2359304 | tf_op jit(solution)/shard_map/ppermute | solution.py:290
  907.9 48.9 %collective-permute-start.18 = (bf16[96,8192]{1,0:T(8,128)(2,1)S(1)}, bf16[96,8192]{1,0:T(8,128)(2,1)S(1)}, u32[]{:S(2)}, u32[]{:S(2)}) collective-permute-start(bf16[96,8192]{1,0:T(8,128)(2,1)S(1)} %constant_dynamic-slice_fusion.4), channel_id=1, source_target_pairs={{0,1},{1,0},{2,3},{3,2},{4,5},{5,4},{6,7},{7,6},{8,9},{9,8},{10,11... | collective-permute-start | bytes 4718600 | tf_op jit(solution)/shard_map/ppermute | solution.py:290
  910.4 48.4 %collective-permute-start.8 = (bf16[48,1536]{1,0:T(8,128)(2,1)S(1)}, bf16[48,1536]{1,0:T(8,128)(2,1)S(1)}, u32[]{:S(2)}, u32[]{:S(2)}) collective-permute-start(bf16[48,1536]{1,0:T(8,128)(2,1)S(1)} %add_convert_fusion.12), channel_id=1, source_target_pairs={{0,2},{1,3},{2,0},{3,1},{4,6},{5,7},{6,4},{7,5},{8,10},{9,11},{10,... | collective-permute-start | bytes 442376 | tf_op jit(solution)/shard_map/ppermute | solution.py:295
  913.9 92.3 %collective-permute-start.13 = (bf16[96,1536]{1,0:T(8,128)(2,1)S(1)}, bf16[96,1536]{1,0:T(8,128)(2,1)S(1)}, u32[]{:S(2)}, u32[]{:S(2)}) collective-permute-start(bf16[96,1536]{1,0:T(8,128)(2,1)S(1)} %pad_maximum_fusion.14), channel_id=1, source_target_pairs={{0,1},{1,0},{2,3},{3,2},{4,5},{5,4},{6,7},{7,6},{8,9},{9,8},{10,11... | collective-permute-start | bytes 884744 | tf_op jit(solution)/shard_map/ppermute | solution.py:295
  915.0 47.1 %collective-permute-start.23 = (bf16[128,1536]{1,0:T(8,128)(2,1)S(1)}, bf16[128,1536]{1,0:T(8,128)(2,1)S(1)}, u32[]{:S(2)}, u32[]{:S(2)}) collective-permute-start(bf16[128,1536]{1,0:T(8,128)(2,1)S(1)} %constant_dynamic-slice_fusion.1), channel_id=1, source_target_pairs={{0,2},{1,3},{2,0},{3,1},{4,6},{5,7},{6,4},{7,5},{8,10},{9,11},{10,... | collective-permute-start | bytes 1179656 | tf_op jit(solution)/shard_map/ppermute | solution.py:290
  957.2 48.6 %collective-permute-start.19 = (bf16[48,8192]{1,0:T(8,128)(2,1)S(1)}, bf16[48,8192]{1,0:T(8,128)(2,1)S(1)}, u32[]{:S(2)}, u32[]{:S(2)}) collective-permute-start(bf16[48,8192]{1,0:T(8,128)(2,1)S(1)} %constant_dynamic-slice_fusion.3), channel_id=1, source_target_pairs={{0,2},{1,3},{2,0},{3,1},{4,6},{5,7},{6,4},{7,5},{8,10},{9,11},{10,... | collective-permute-start | bytes 2359304 | tf_op jit(solution)/shard_map/ppermute | solution.py:290
  958.8 89.5 %collective-permute-start.9 = (bf16[96,1536]{1,0:T(8,128)(2,1)S(1)}, bf16[96,1536]{1,0:T(8,128)(2,1)S(1)}, u32[]{:S(2)}, u32[]{:S(2)}) collective-permute-start(bf16[96,1536]{1,0:T(8,128)(2,1)S(1)} %pad_maximum_fusion.13), channel_id=1, source_target_pairs={{0,1},{1,0},{2,3},{3,2},{4,5},{5,4},{6,7},{7,6},{8,9},{9,8},{10,11... | collective-permute-start | bytes 884744 | tf_op jit(solution)/shard_map/ppermute | solution.py:295
  962.2 68.9 %collective-permute-start.24 = (bf16[128,1536]{1,0:T(8,128)(2,1)S(1)}, bf16[128,1536]{1,0:T(8,128)(2,1)S(1)}, u32[]{:S(2)}, u32[]{:S(2)}) collective-permute-start(bf16[128,1536]{1,0:T(8,128)(2,1)S(1)} %add_convert_fusion.4), channel_id=1, source_target_pairs={{0,2},{1,3},{2,0},{3,1},{4,6},{5,7},{6,4},{7,5},{8,10},{9,11},{10,... | collective-permute-start | bytes 1179656 | tf_op jit(solution)/shard_map/ppermute | solution.py:295
  1006.0 42.0 %collective-permute-start.20 = (bf16[48,8192]{1,0:T(8,128)(2,1)S(1)}, bf16[48,8192]{1,0:T(8,128)(2,1)S(1)}, u32[]{:S(2)}, u32[]{:S(2)}) collective-permute-start(bf16[48,8192]{1,0:T(8,128)(2,1)S(1)} %add_convert_fusion.2), channel_id=1, source_target_pairs={{0,2},{1,3},{2,0},{3,1},{4,6},{5,7},{6,4},{7,5},{8,10},{9,11},{10,... | collective-permute-start | bytes 2359304 | tf_op jit(solution)/shard_map/ppermute | solution.py:295
  1048.2 50.2 %collective-permute-start.21 = (bf16[96,8192]{1,0:T(8,128)(2,1)S(1)}, bf16[96,8192]{1,0:T(8,128)(2,1)S(1)}, u32[]{:S(2)}, u32[]{:S(2)}) collective-permute-start(bf16[96,8192]{1,0:T(8,128)(2,1)S(1)} %pad_maximum_fusion.7), channel_id=1, source_target_pairs={{0,1},{1,0},{2,3},{3,2},{4,5},{5,4},{6,7},{7,6},{8,9},{9,8},{10,11... | collective-permute-start | bytes 4718600 | tf_op jit(solution)/shard_map/ppermute | solution.py:295
  (40 other events, 811.3 us)
Sparse Core Ops, SparseCore 0:
  10.4 41.6 all-gather.7
  54.6 38.7 all-gather.5
  95.3 38.7 all-gather.9
  135.9 125.1 all-gather.11
  262.8 71.9 all-gather.13
  404.8 63.4 reduce-scatter.9
  540.1 53.0 reduce-scatter.7
  596.7 53.9 reduce-scatter.5
  654.2 92.2 reduce-scatter.13
  750.0 156.3 reduce-scatter.11
